TPU v7x, 128 devices: a whole 4x4x4 slice. The times are simulated.
128 devices in a mesh: rows: 8 (over x, z_lo), cols: 16 (over z_hi, y, core).
Axes of the slice: x: 4, y: 4, z: 4 (z_hi: 2, z_lo: 2; z = z_hi * 2 + z_lo), core: 2. Of those that a mesh axis runs over, the one named last changes fastest.
Arguments:
- ancestor_inv: bfloat16 [16384, 16384], P('rows', 'cols'), may hold values from -0.0625 to 0.0625
- lfactor: bfloat16 [32, 256, 6, 256], P('cols'), may hold values from -0.8984375 to 0.8984375
- struct: int32 [6, 32], replicated, may hold values from 0 to 63, as said below
- validity: int32 [6, 32], replicated, may hold values from 0 to 1, as said below
- diag_inverse: float32 [6, 256, 256], replicated, may hold values from -6 to 6
Outputs:
- column_block: bfloat16 [16384, 1536], P(('rows', 'cols'))
- diagonal_block: float32 [6, 256, 256], replicated
Inputs may be any that keep to these rules, and one draw needn't show every extreme that they name: `struct`: within a supernode the 32 tile indices are distinct and increasing, and every list holds tiles 0 and 63. `validity`: every tile index of 0 to 63 is a valid entry of some supernode's list; some supernode has all 32 flags set.
All inputs are finite; a program needn't handle non-finite values.
Results may differ from a plain program's by a relative error of at most 0.001.
Values may be sent and summed in bfloat16 or wider, within the bound.
No kernel may reach another device: no remote copies, remote signals or barrier semaphores. Data moves between devices by JAX's collectives and lax.ppermute only.
A program may use at most 192 MiB of HBM per device.

v0:
```python
import jax
import jax.numpy as jnp
from jax import lax
from jax.experimental import pallas as pl
from jax.experimental.pallas import tpu as pltpu
from jax.sharding import Mesh, PartitionSpec as P


BF16 = jnp.bfloat16
F32 = jnp.float32
I16 = jnp.int16
NX, NL, NH, NY, NC = 4, 2, 2, 4, 2
XL = ("x", "l")
HY = ("h", "y")
CHIPS = XL + HY
CORE_SWAP = [(0, 1), (1, 0)]
UP = [(i, (i + 1) % NX) for i in range(NX)]
DOWN = [(i, (i - 1) % NX) for i in range(NX)]
LEVELS = 32000.0
LOWEST = -100.0
LANES = 128


def level_of(top):
    return jnp.maximum(jnp.ceil(jnp.log2(jnp.maximum(top, 1e-37)) + 0.01), LOWEST)


def code(values, level):
    return jnp.round(values * (jnp.exp2(-level) * LEVELS)).astype(jnp.int32).astype(I16)


def plain(coded):
    return coded.astype(jnp.int32).astype(F32)


def scale_of(level):
    return jnp.exp2(level) * (1.0 / LEVELS)


def share_kernel(where, l_ref, o_ref, buffer, sem):
    part = o_ref.shape[3]
    copy = pltpu.make_async_copy(
        l_ref.at[:, :, pl.ds(pl.multiple_of(where[2] * part, part), part)], buffer, sem
    )
    copy.start()
    copy.wait()
    members = o_ref.shape[2]
    for i in range(o_ref.shape[0]):
        core = i % NC
        o_ref[i] = buffer[:, core * members : (core + 1) * members]


def stage_kernel(where, own_ref, other_ref, o_ref, sems):
    core = where[1]
    copies = [
        pltpu.make_async_copy(own_ref, o_ref.at[core], sems.at[0]),
        pltpu.make_async_copy(other_ref, o_ref.at[1 - core], sems.at[1]),
    ]
    for copy in copies:
        copy.start()
    for copy in copies:
        copy.wait()


def pick_kernel(place, where, x_ref, window_ref, own_ref):
    members, window = window_ref.shape[:2]
    groups = own_ref.shape[0]
    chip, core = where[0], where[1]
    for k in range(members):

        def tile(t):
            p = place[core * members + k, t]
            block = x_ref[jnp.maximum(p, 0), k]
            return jnp.where(p >= 0, block, jnp.zeros_like(block))

        for s in range(window):
            window_ref[k, s] = tile(chip * window + s)
        for g in range(groups):
            own_ref[g, k] = tile(g * window + chip)


def product_kernel(place, where, a_ref, *refs):
    inputs = NL * NX
    parts, outs = refs[:inputs], refs[inputs : inputs + NH * NY]
    panel, order, sems = refs[inputs + NH * NY :]
    members, window, _, _, size = panel.shape
    half = window // NC
    chip, core, group, x, l, h, y = (where[i] for i in range(7))
    step = pl.program_id(0)
    tile = group * window + lax.rem(h + step // NY, NH) * NY + lax.rem(y + step, NY)

    @pl.when(step == 0)
    def _():
        copies = []
        for side in range(NL):
            for hop, shift in enumerate(RING):
                source = lax.rem(x + shift, NX) * NL + lax.rem(l + side, NL)
                i = side * NX + hop
                copies.append(pltpu.make_async_copy(parts[i], panel.at[:, :, source], sems.at[i]))
        for copy in copies:
            copy.start()
        for k in range(members):
            listed = [place[core * members + k, chip * window + s] >= 0 for s in range(window)]
            count = sum(jnp.where(f, 1, 0) for f in listed)
            order[k, window] = count
            front, back = jnp.int32(0), count
            for s in range(window):
                order[k, jnp.where(listed[s], front, back)] = s
                front = front + jnp.where(listed[s], 1, 0)
                back = back + jnp.where(listed[s], 0, 1)
        for copy in copies:
            copy.wait()

    for k in range(members):
        cols = slice(k * size, (k + 1) * size)
        wanted = place[core * members + k, tile] >= 0
        few = order[k, window] <= half

        def store(values):
            for j, out in enumerate(outs):

                @pl.when(step == j)
                def _():
                    out[:, cols] = values

        def finish(tiles):
            values = jnp.zeros((size, size), F32)
            for s in tiles:
                start = pl.multiple_of(lax.rem(s, half) * size, size)
                left = a_ref[lax.div(s, half), :, pl.ds(start, size)]
                values += jnp.dot(left, panel[k, s].reshape(size, size), preferred_element_type=F32)
            level = level_of(jnp.max(jnp.abs(values), axis=0, keepdims=True))
            tail = jnp.broadcast_to(level, (16, size)).astype(jnp.int32).astype(I16)
            store(jnp.concatenate([code(values, level), tail], axis=0))

        @pl.when(jnp.logical_and(wanted, few))
        def _():
            finish([order[k, i] for i in range(half)])

        @pl.when(jnp.logical_and(wanted, jnp.logical_not(few)))
        def _():
            finish([jnp.int32(s) for s in range(window)])

        @pl.when(jnp.logical_not(wanted))
        def _():
            store(jnp.zeros((size + 16, size), I16))


def diagonal_kernel(place, where, *refs):
    count = NH * NY
    coded, parts, (d_ref, block) = refs[:count], refs[count : 2 * count], refs[2 * count :]
    _, members, _, size = parts[0].shape
    core, group, h, y = where[1], where[2], where[5], where[6]
    block[...] = jnp.zeros_like(block)
    for side in range(NH):
        for hop, shift in enumerate(RING):
            tile = lax.rem(h + side, NH) * NY + lax.rem(y + shift, NY)
            q_ref, ref = coded[side * NY + shift], parts[side * NY + hop]
            for k in range(members):
                cols = slice(k * size, (k + 1) * size)

                @pl.when(place[core * members + k, group * count + tile] >= 0)
                def _():
                    own = ref[:, k].reshape(size, size)
                    rest = plain(q_ref[:size, cols])
                    high = rest.astype(BF16)
                    low = (rest - high.astype(F32)).astype(BF16)
                    total = sum(
                        lax.dot_general(
                            own, term, (((0,), (0,)), ((), ())), preferred_element_type=F32
                        )
                        for term in (high, low)
                    )
                    block[:, cols] -= total * scale_of(plain(q_ref[size : size + 16, cols])[:1])

    values = block[...]
    level = level_of(jnp.max(jnp.abs(values), keepdims=True))
    width = values.shape[1] // 2
    for i in range(2):
        d_ref[i, :, :width] = code(values[:, i * width : (i + 1) * width], level)
        d_ref[i, :, width:] = jnp.broadcast_to(level, (size, LANES)).astype(jnp.int32).astype(I16)


def finish_kernel(place, where, *refs):
    parts, (u_ref, swap_ref) = refs[:-2], refs[-2:]
    sources = len(parts)
    slab, width = u_ref.shape
    size = 2 * slab
    members = width // size
    chip, core, group = where[0], where[1], where[2]
    mine = group * sources + chip
    for k in range(members):
        cols = slice(k * size, (k + 1) * size)
        total = jnp.zeros((size, size), F32)
        for ref in parts:
            scale = scale_of(plain(ref[size : size + 16, cols])[:1])
            total += plain(ref[:size, cols]) * scale
        keep = place[core * members + k, mine] >= 0
        rounded = jnp.where(keep, -total, jnp.zeros_like(total)).astype(BF16)
        first = core == 0
        u_ref[:, cols] = jnp.where(first, rounded[:slab], rounded[slab:])
        swap_ref[:, cols] = jnp.where(first, rounded[slab:], rounded[:slab])


def piece_kernel(q_ref, inverse_ref, o_ref):
    width = q_ref.shape[2] - LANES
    scale = scale_of(plain(q_ref[:, :, width:]))
    sums = [
        jnp.sum(plain(q_ref[:, :, i : i + LANES]) * scale, axis=0) for i in range(0, width, LANES)
    ]
    values = inverse_ref[...] - jnp.concatenate(sums, axis=1)
    level = level_of(jnp.max(jnp.abs(values), keepdims=True))
    coded = jnp.concatenate(
        [
            code(values, level),
            jnp.broadcast_to(level, (values.shape[0], LANES)).astype(jnp.int32).astype(I16),
        ],
        axis=1,
    )
    for j in range(o_ref.shape[0]):
        o_ref[j] = coded


def total_kernel(q_ref, o_ref):
    pieces, cores, depth, reach = q_ref.shape
    supers, size, _ = o_ref.shape
    width = reach - LANES
    count = pieces // 2
    for c in range(cores):
        for i in range(2):
            rows = slice(i * count, (i + 1) * count)
            scale = scale_of(plain(q_ref[rows, c, :, width:]))
            for t in range(width // LANES):
                lane = (i * width + t * LANES) % size
                k = c * (supers // cores) + (i * width + t * LANES) // size
                values = plain(q_ref[rows, c, :, t * LANES : (t + 1) * LANES]) * scale
                o_ref[k, :, lane : lane + LANES] = values.reshape(count * depth, LANES)


def spread(own, axis, up):
    below = lax.ppermute(own, axis, UP)
    above = lax.ppermute(own, axis, DOWN)
    far = lax.ppermute(below, axis, UP) if up else lax.ppermute(above, axis, DOWN)
    return [own, below, above, far]


RING = (0, 3, 1, 2)


def update(ancestor_inv, lfactor, struct, validity, diag_inverse):
    rows, cols = ancestor_inv.shape
    entries, size, supers, _ = lfactor.shape
    groups = NX * NL
    chips = NH * NY
    part = size // groups
    members = supers // NC
    width = members * size
    group = lax.axis_index(XL)
    chip = lax.axis_index(HY)
    core = lax.axis_index("c")
    listed = struct.shape[1]
    tiles = rows * groups // size
    window = tiles // chips
    smem = pl.BlockSpec(memory_space=pltpu.SMEM)
    vmem = pl.BlockSpec(memory_space=pltpu.VMEM)

    other = lax.ppermute(ancestor_inv, "c", CORE_SWAP)

    hits = (struct[:, :, None] == jnp.arange(tiles, dtype=jnp.int32)) & (validity[:, :, None] > 0)
    position = jnp.arange(listed, dtype=jnp.int32)[None, :, None]
    place = jnp.max(jnp.where(hits, position, -1), axis=1)
    where = jnp.stack([chip, core, group] + [lax.axis_index(a) for a in ("x", "l", "h", "y")])

    share = pl.pallas_call(
        share_kernel,
        out_shape=jax.ShapeDtypeStruct((chips * NC, entries, members, part, size), BF16),
        in_specs=[smem, pl.BlockSpec(memory_space=pltpu.HBM)],
        out_specs=vmem,
        scratch_shapes=[
            pltpu.VMEM((entries, supers, part, size), BF16),
            pltpu.SemaphoreType.DMA,
        ],
        name="share",
    )(where, jnp.transpose(lfactor, (0, 2, 1, 3)))
    share = lax.all_to_all(share, ("h", "y", "c"), split_axis=0, concat_axis=0, tiled=True)
    share = share.reshape(listed, members, part, size)

    block = jax.ShapeDtypeStruct((members, window, part, size), BF16)
    near, own = pl.pallas_call(
        pick_kernel,
        out_shape=[block, jax.ShapeDtypeStruct((groups, members, part, size), BF16)],
        in_specs=[smem, smem, vmem],
        out_specs=[vmem] * 2,
        compiler_params=pltpu.CompilerParams(vmem_limit_bytes=8 << 20),
        name="pick",
    )(place, where, share)
    across = lax.ppermute(near, "l", CORE_SWAP)
    window_parts = spread(near, "x", True)
    window_parts += spread(across, "x", False)
    own = lax.all_to_all(own, XL, split_axis=0, concat_axis=0, tiled=True)
    across = lax.ppermute(own, "h", CORE_SWAP)
    row_parts = spread(own, "y", True)
    row_parts += spread(across, "y", False)

    staged = pl.pallas_call(
        stage_kernel,
        out_shape=jax.ShapeDtypeStruct((NC, rows, cols), BF16),
        in_specs=[smem, pl.BlockSpec(memory_space=pl.ANY), pl.BlockSpec(memory_space=pl.ANY)],
        out_specs=pl.BlockSpec(memory_space=pl.ANY),
        scratch_shapes=[pltpu.SemaphoreType.DMA((2,))],
        compiler_params=pltpu.CompilerParams(vmem_limit_bytes=1 << 20),
        name="stage",
    )(where, ancestor_inv, other)

    def row_tile(j, _, where):
        return 0, lax.rem(where[5] + j // NY, NH) * NY + lax.rem(where[6] + j, NY), 0

    coded = pl.pallas_call(
        product_kernel,
        out_shape=[jax.ShapeDtypeStruct((size + 16, width), I16)] * chips,
        grid_spec=pltpu.PrefetchScalarGridSpec(
            num_scalar_prefetch=2,
            grid=(chips,),
            in_specs=[pl.BlockSpec((NC, size, cols), row_tile)]
            + [pl.BlockSpec(memory_space=pltpu.HBM)] * len(window_parts),
            out_specs=[vmem] * chips,
            scratch_shapes=[
                pltpu.VMEM((members, window, groups, part, size), BF16),
                pltpu.SMEM((members, window + 1), jnp.int32),
                pltpu.SemaphoreType.DMA((len(window_parts),)),
            ],
        ),
        compiler_params=pltpu.CompilerParams(vmem_limit_bytes=20 << 20),
        name="product",
    )(place, where, staged, *window_parts)
    pieces = groups * chips
    depth = 2 * size // pieces
    reach = width // 2 + LANES
    diag = pl.pallas_call(
        diagonal_kernel,
        out_shape=jax.ShapeDtypeStruct((2, size, reach), I16),
        in_specs=[smem, smem] + [vmem] * (chips + len(row_parts)),
        out_specs=vmem,
        scratch_shapes=[pltpu.VMEM((size, width), F32)],
        compiler_params=pltpu.CompilerParams(vmem_limit_bytes=16 << 20),
        name="diagonal",
    )(place, where, *coded, *row_parts)

    sums = [coded[0]]
    for shifts in ((6, 5, 7), (2, 4, 1, 3)):
        for j in shifts:
            to = [
                (h * NY + y, (h + j // NY) % NH * NY + (y + j) % NY)
                for h in range(NH)
                for y in range(NY)
            ]
            sums.append(lax.ppermute(coded[j], HY, to))
    slab = jax.ShapeDtypeStruct((size // NC, width), BF16)
    mine, theirs = pl.pallas_call(
        finish_kernel,
        out_shape=[slab, slab],
        in_specs=[smem, smem] + [vmem] * len(sums),
        out_specs=[vmem] * 2,
        compiler_params=pltpu.CompilerParams(vmem_limit_bytes=12 << 20),
        name="finish",
    )(place, where, *sums)

    theirs = lax.ppermute(theirs, "c", CORE_SWAP)
    column_block = jnp.where(
        core == 0,
        jnp.concatenate([mine, theirs], axis=1),
        jnp.concatenate([theirs, mine], axis=1),
    )

    diag = diag.reshape(pieces, depth, reach)
    diag = lax.all_to_all(diag, CHIPS, split_axis=0, concat_axis=0, tiled=True)
    index = group * chips + chip
    inverse = lax.dynamic_slice(
        diag_inverse,
        (core * members, index % (pieces // 2) * depth, 0),
        (members, depth, size),
    )
    inverse = jnp.transpose(inverse, (1, 0, 2)).reshape(depth, 2, width // 2)
    inverse = lax.dynamic_index_in_dim(inverse, index // (pieces // 2), 1, keepdims=False)
    piece = pl.pallas_call(
        piece_kernel,
        out_shape=jax.ShapeDtypeStruct((pieces * NC, depth, reach), I16),
        in_specs=[vmem, vmem],
        out_specs=vmem,
        compiler_params=pltpu.CompilerParams(vmem_limit_bytes=6 << 20),
        name="piece",
    )(diag, inverse)
    whole = lax.all_to_all(piece, CHIPS + ("c",), split_axis=0, concat_axis=0, tiled=True)
    diagonal = pl.pallas_call(
        total_kernel,
        out_shape=jax.ShapeDtypeStruct(diag_inverse.shape, F32),
        in_specs=[vmem],
        out_specs=vmem,
        compiler_params=pltpu.CompilerParams(vmem_limit_bytes=12 << 20),
        name="total",
    )(whole.reshape(pieces, NC, depth, reach))
    return column_block, diagonal


def solution(mesh):
    fine = Mesh(mesh.devices.reshape(NX, NL, NH, NY, NC), ("x", "l", "h", "y", "c"))
    return jax.shard_map(
        update,
        mesh=fine,
        in_specs=(P(XL, ("h", "y", "c")), P(("h", "y", "c")), P(), P(), P()),
        out_specs=(P(("x", "l", "h", "y", "c")), P()),
        check_vma=False,
    )
```

profile of v0, /device:TPU:1, one launch (start us, length us, event | category | flops | bytes accessed | tf_op | source)
XLA Modules:
  0.0 197.8 jit_solution(859842905937368080)
XLA Ops:
  0.6 1.5 collective-permute-start
  2.1 0.6 stack.31.where
  2.7 2.8 %share.1 = bf16[16,2,3,32,256]{4,3,2,1,0:T(8,128)(2,1)} custom-call(s32[7]{0:T(128)} %stack.31.where, bf16[2,6,256,256]{3,2,1,0:T(8,128)(2,1)} %bitcast.18), custom_call_target="tpu_custom_call" | custom-call | tf_op jit(solution)/shard_map/share/pallas_call | solution.py:274
  5.6 8.0 %all-to-all-start = ((bf16[16,2,3,32,256]{4,3,2,1,0:T(8,128)(2,1)}), bf16[16,2,3,32,256]{4,3,2,1,0:T(8,128)(2,1)S(1)}, u32[]{:S(2)}, u32[]{:S(2)}) async-start(bf16[16,2,3,32,256]{4,3,2,1,0:T(8,128)(2,1)} %share.1), calls=%async_computation | async-start | bytes 3145728 | tf_op jit(solution)/shard_map/all_to_all | solution.py:285
  13.8 22.7 %all-to-all-done = bf16[16,2,3,32,256]{4,3,2,1,0:T(8,128)(2,1)S(1)} async-done(((bf16[16,2,3,32,256]{4,3,2,1,0:T(8,128)(2,1)}), bf16[16,2,3,32,256]{4,3,2,1,0:T(8,128)(2,1)S(1)}, u32[]{:S(2)}, u32[]{:S(2)}) %all-to-all-start) | async-done | bytes 1572896 | tf_op jit(solution)/shard_map/all_to_all | solution.py:285
  36.5 0.8 pick.1
  37.3 0.7 copy-done.11
  38.1 1.2 collective-permute-start.1
  39.3 4.2 %all-to-all-start.1 = ((bf16[8,3,32,256]{3,2,1,0:T(8,128)(2,1)}), bf16[8,3,32,256]{3,2,1,0:T(8,128)(2,1)S(1)}, u32[]{:S(2)}, u32[]{:S(2)}) async-start(bf16[8,3,32,256]{3,2,1,0:T(8,128)(2,1)} %copy-done.11), calls=%async_computation.1 | async-start | bytes 786432 | tf_op jit(solution)/shard_map/all_to_all | solution.py:300
  43.4 2.7 %collective-permute-start.2 = (bf16[3,8,32,256]{3,2,1,0:T(8,128)(2,1)S(1)}, bf16[3,8,32,256]{3,2,1,0:T(8,128)(2,1)S(1)}, u32[]{:S(2)}, u32[]{:S(2)}) collective-permute-start(bf16[3,8,32,256]{3,2,1,0:T(8,128)(2,1)S(1)} %get-tuple-element.14.refs_0_), channel_id=1, source_target_pairs={{0,96},{32,0},{64,32},{96,64},{1,97},{33,1},{65,33},{97,65},{2,98}... | collective-permute-start | bytes 1179656 | tf_op jit(solution)/shard_map/ppermute | solution.py:242
  46.1 1.2 collective-permute-start.4
  47.3 6.8 %all-to-all-done.1.refs_8_ = bf16[8,3,32,256]{3,2,1,0:T(8,128)(2,1)S(1)} async-done(((bf16[8,3,32,256]{3,2,1,0:T(8,128)(2,1)}), bf16[8,3,32,256]{3,2,1,0:T(8,128)(2,1)S(1)}, u32[]{:S(2)}, u32[]{:S(2)}) %all-to-all-start.1) | async-done | bytes 393248 | tf_op jit(solution)/shard_map/all_to_all | solution.py:300
  54.1 1.4 collective-permute-start.19
  55.6 1.7 collective-permute-done.2.refs_2_
  57.3 1.2 collective-permute-start.3
  58.8 1.9 collective-permute-start.6
  60.7 3.4 %collective-permute-done.16.refs_9_ = bf16[8,3,32,256]{3,2,1,0:T(8,128)(2,1)S(1)} collective-permute-done((bf16[8,3,32,256]{3,2,1,0:T(8,128)(2,1)S(1)}, bf16[8,3,32,256]{3,2,1,0:T(8,128)(2,1)S(1)}, u32[]{:S(2)}, u32[]{:S(2)}) %collective-permute-start.16) | collective-permute-done | bytes 393248 | tf_op jit(solution)/shard_map/ppermute | solution.py:241
  64.2 3.1 %collective-permute-done.19.refs_12_ = bf16[8,3,32,256]{3,2,1,0:T(8,128)(2,1)S(1)} collective-permute-done((bf16[8,3,32,256]{3,2,1,0:T(8,128)(2,1)S(1)}, bf16[8,3,32,256]{3,2,1,0:T(8,128)(2,1)S(1)}, u32[]{:S(2)}, u32[]{:S(2)}) %collective-permute-start.19) | collective-permute-done | bytes 393248 | tf_op jit(solution)/shard_map/ppermute | solution.py:301
  67.3 2.9 %collective-permute-start.17 = (bf16[8,3,32,256]{3,2,1,0:T(8,128)(2,1)S(1)}, bf16[8,3,32,256]{3,2,1,0:T(8,128)(2,1)S(1)}, u32[]{:S(2)}, u32[]{:S(2)}) collective-permute-start(bf16[8,3,32,256]{3,2,1,0:T(8,128)(2,1)S(1)} %all-to-all-done.1.refs_8_), channel_id=1, source_target_pairs={{0,6},{2,0},{4,2},{6,4},{1,7},{3,1},{5,3},{7,5},{8,14},{10,8},{12,... | collective-permute-start | bytes 1179656 | tf_op jit(solution)/shard_map/ppermute | solution.py:242
  70.2 0.7 collective-permute-start.7
  70.9 5.3 %collective-permute-done.5.refs_5_ = bf16[3,8,32,256]{3,2,1,0:T(8,128)(2,1)S(1)} collective-permute-done((bf16[3,8,32,256]{3,2,1,0:T(8,128)(2,1)}, bf16[3,8,32,256]{3,2,1,0:T(8,128)(2,1)S(1)}, u32[]{:S(2)}, u32[]{:S(2)}) %collective-permute-start.5) | collective-permute-done | bytes 393248 | tf_op jit(solution)/shard_map/ppermute | solution.py:241
  76.2 1.6 collective-permute-start.18
  77.8 1.3 collective-permute-start.22
  79.2 2.2 %copy-done.1 = bf16[2048,1024]{1,0:T(8,128)(2,1)S(1)} copy-done((bf16[2048,1024]{1,0:T(8,128)(2,1)S(1)}, bf16[2048,1024]{1,0:T(8,128)(2,1)}, u32[]{:S(2)}) %copy-start.1) | copy-done | bytes 4194328
  81.4 3.0 %stage.1.a_ref = bf16[2,2048,1024]{2,1,0:T(8,128)(2,1)S(1)} custom-call(s32[7]{0:T(128)S(1)} %copy-done.13, bf16[2048,1024]{1,0:T(8,128)(2,1)S(1)} %copy-done.1, bf16[2048,1024]{1,0:T(8,128)(2,1)} %collective-permute-done.other_ref), custom_call_target="tpu_custom_call" | custom-call | tf_op jit(solution)/shard_map/stage/pallas_call | solution.py:305
  84.4 1.0 copy-done.8
  85.4 1.0 copy-done.10
  86.4 8.1 %product.1 = (s16[272,768]{1,0:T(8,128)(2,1)S(1)}, s16[272,768]{1,0:T(8,128)(2,1)S(1)}, s16[272,768]{1,0:T(8,128)(2,1)S(1)}, s16[272,768]{1,0:T(8,128)(2,1)S(1)}...) custom-call(s32[6,64]{1,0:T(8,128)S(1)} %select_reduce_fusion.place,, ...), custom_call_target="tpu_custom_call" | custom-call | tf_op jit(solution)/shard_map/product/pallas_call | solution.py:318
  94.7 4.6 %diagonal.1 = s16[2,256,512]{2,1,0:T(8,128)(2,1)} custom-call(s32[6,64]{1,0:T(8,128)S(1)} %select_reduce_fusion.place, s32[7]{0:T(128)S(1)} %copy-done.13, s16[272,768]{1,0:T(8,128)(2,1)S(1)} %get-tuple-element.15.refs_0_, s16[272,768]{1,0:T(8,128)(2,1)S(1)} %get-tuple-element.21.refs_1_, s16[272,768]{1,0:T(8,128)(2,1)S(1)} %get-tuple-element.19.refs_2_, ...), custom_call_target="tpu_custom_call" | custom-call | tf_op jit(solution)/shard_map/diagonal/pallas_call | solution.py:339
  99.4 12.7 %all-to-all-start.2 = ((s16[64,8,512]{2,1,0:T(8,128)(2,1)}), s16[64,8,512]{2,1,0:T(8,128)(2,1)S(1)}, u32[]{:S(2)}, u32[]{:S(2)}) async-start(s16[64,8,512]{2,1,0:T(8,128)(2,1)} %bitcast.9), calls=%async_computation.2 | async-start | bytes 1048576 | tf_op jit(solution)/shard_map/all_to_all | solution.py:376
  112.1 5.0 %collective-permute-start.8 = (s16[272,768]{1,0:T(8,128)(2,1)}, s16[272,768]{1,0:T(8,128)(2,1)}, u32[]{:S(2)}, u32[]{:S(2)}) collective-permute-start(s16[272,768]{1,0:T(8,128)(2,1)} %get-tuple-element.16.refs_6_), channel_id=1, source_target_pairs={{0,12},{2,14},{4,8},{6,10},{8,4},{10,6},{12,0},{14,2},{1,13},{3,15... | collective-permute-start | bytes 1253384 | tf_op jit(solution)/shard_map/ppermute | solution.py:357
  117.4 6.5 %all-to-all-done.2.q_ref = s16[64,8,512]{2,1,0:T(8,128)(2,1)S(1)} async-done(((s16[64,8,512]{2,1,0:T(8,128)(2,1)}), s16[64,8,512]{2,1,0:T(8,128)(2,1)S(1)}, u32[]{:S(2)}, u32[]{:S(2)}) %all-to-all-start.2) | async-done | bytes 524320 | tf_op jit(solution)/shard_map/all_to_all | solution.py:376
  123.8 0.4 piece.1
  124.2 1.0 copy-done.2
  125.2 22.6 %all-to-all-start.3 = ((s16[128,8,512]{2,1,0:T(8,128)(2,1)}), s16[128,8,512]{2,1,0:T(8,128)(2,1)S(1)}, u32[]{:S(2)}, u32[]{:S(2)}) async-start(s16[128,8,512]{2,1,0:T(8,128)(2,1)} %copy-done.2), calls=%async_computation.3 | async-start | bytes 2097152 | tf_op jit(solution)/shard_map/all_to_all | solution.py:393
  147.8 5.6 %collective-permute-start.10 = (s16[272,768]{1,0:T(8,128)(2,1)}, s16[272,768]{1,0:T(8,128)(2,1)S(1)}, u32[]{:S(2)}, u32[]{:S(2)}) collective-permute-start(s16[272,768]{1,0:T(8,128)(2,1)} %copy-done.6), channel_id=1, source_target_pairs={{0,14},{2,8},{4,10},{6,12},{8,6},{10,0},{12,2},{14,4},{1,15},{3,9}... | collective-permute-start | bytes 1253384 | tf_op jit(solution)/shard_map/ppermute | solution.py:357
  153.5 0.4 collective-permute-start.11
  154.1 0.5 collective-permute-start.13
  154.6 2.2 %collective-permute-start.14 = (s16[272,768]{1,0:T(8,128)(2,1)S(1)}, s16[272,768]{1,0:T(8,128)(2,1)S(1)}, u32[]{:S(2)}, u32[]{:S(2)}) collective-permute-start(s16[272,768]{1,0:T(8,128)(2,1)S(1)} %get-tuple-element.22.refs_3_), channel_id=1, source_target_pairs={{0,6},{2,0},{4,2},{6,4},{8,14},{10,8},{12,10},{14,12},{1,7},{3,1},... | collective-permute-start | bytes 1253384 | tf_op jit(solution)/shard_map/ppermute | solution.py:357
  156.8 16.6 %collective-permute-done.10.refs_3_ = s16[272,768]{1,0:T(8,128)(2,1)S(1)} collective-permute-done((s16[272,768]{1,0:T(8,128)(2,1)}, s16[272,768]{1,0:T(8,128)(2,1)S(1)}, u32[]{:S(2)}, u32[]{:S(2)}) %collective-permute-start.10) | collective-permute-done | bytes 417824 | tf_op jit(solution)/shard_map/ppermute | solution.py:357
  173.4 9.4 %collective-permute-done.12.refs_5_ = s16[272,768]{1,0:T(8,128)(2,1)S(1)} collective-permute-done((s16[272,768]{1,0:T(8,128)(2,1)}, s16[272,768]{1,0:T(8,128)(2,1)S(1)}, u32[]{:S(2)}, u32[]{:S(2)}) %collective-permute-start.12) | collective-permute-done | bytes 417824 | tf_op jit(solution)/shard_map/ppermute | solution.py:357
  182.8 6.1 %collective-permute-done.14.refs_7_ = s16[272,768]{1,0:T(8,128)(2,1)S(1)} collective-permute-done((s16[272,768]{1,0:T(8,128)(2,1)S(1)}, s16[272,768]{1,0:T(8,128)(2,1)S(1)}, u32[]{:S(2)}, u32[]{:S(2)}) %collective-permute-start.14) | collective-permute-done | bytes 417824 | tf_op jit(solution)/shard_map/ppermute | solution.py:357
  188.9 2.7 %finish.1 = (bf16[128,768]{1,0:T(8,128)(2,1)S(1)}, bf16[128,768]{1,0:T(8,128)(2,1)}) custom-call(s32[6,64]{1,0:T(8,128)S(1)} %select_reduce_fusion.place, s32[7]{0:T(128)S(1)} %copy-done.13, s16[272,768]{1,0:T(8,128)(2,1)S(1)} %get-tuple-element.15.refs_0_, s16[272,768]{1,0:T(8,128)(2,1)} %collective-permute-done.8.refs_1_, ...), custom_call_target="tpu_custom_call" | custom-call | tf_op jit(solution)/shard_map/finish/pallas_call | solution.py:359
  191.6 0.7 copy-done.12
  192.3 1.0 collective-permute-start.15
  193.3 1.3 collective-permute-done.15
  194.5 1.9 maximum_select_fusion
  196.4 1.4 total.1
  (52 shorter events, 1.1 us)
Async XLA Ops:
  0.6 116.7 %copy-start = (f32[6,256,256]{2,1,0:T(8,128)S(1)}, f32[6,256,256]{2,1,0:T(8,128)}, u32[]{:S(2)}) copy-start(f32[6,256,256]{2,1,0:T(8,128)} %param.9) | copy-start | bytes 4718596
  0.6 77.2 %collective-permute-start = (bf16[2048,1024]{1,0:T(8,128)(2,1)}, bf16[2048,1024]{1,0:T(8,128)(2,1)}, u32[]{:S(2)}, u32[]{:S(2)}) collective-permute-start(bf16[2048,1024]{1,0:T(8,128)(2,1)} %own_ref.1), channel_id=1, source_target_pairs={{0,1},{1,0},{2,3},{3,2},{4,5},{5,4},{6,7},{7,6},{8,9},{9,8},{10,11... | collective-permute-start | bytes 12582920 | tf_op jit(solution)/shard_map/ppermute | solution.py:267
  5.6 8.1 %copy-start.14 = (s32[6,32]{1,0:T(8,128)S(1)}, s32[6,32]{1,0:T(8,128)}, u32[]{:S(2)}) copy-start(s32[6,32]{1,0:T(8,128)} %param.8) | copy-start | bytes 2308
  5.6 8.1 %copy-start.15 = (s32[6,32]{1,0:T(8,128)S(1)}, s32[6,32]{1,0:T(8,128)}, u32[]{:S(2)}) copy-start(s32[6,32]{1,0:T(8,128)} %param.7) | copy-start | bytes 2308
  5.6 30.9 %copy-start.13 = (s32[7]{0:T(128)S(1)}, s32[7]{0:T(128)}, u32[]{:S(2)}) copy-start(s32[7]{0:T(128)} %stack.31.where) | copy-start | bytes 88
  5.6 30.9 %all-to-all-start = ((bf16[16,2,3,32,256]{4,3,2,1,0:T(8,128)(2,1)}), bf16[16,2,3,32,256]{4,3,2,1,0:T(8,128)(2,1)S(1)}, u32[]{:S(2)}, u32[]{:S(2)}) async-start(bf16[16,2,3,32,256]{4,3,2,1,0:T(8,128)(2,1)} %share.1), calls=%async_computation | async-start | bytes 3145728 | tf_op jit(solution)/shard_map/all_to_all | solution.py:285
  37.3 0.7 copy-start.11
  38.1 16.1 %collective-permute-start.1 = (bf16[3,8,32,256]{3,2,1,0:T(8,128)(2,1)S(1)}, bf16[3,8,32,256]{3,2,1,0:T(8,128)(2,1)S(1)}, u32[]{:S(2)}, u32[]{:S(2)}) collective-permute-start(bf16[3,8,32,256]{3,2,1,0:T(8,128)(2,1)S(1)} %get-tuple-element.14.refs_0_), channel_id=1, source_target_pairs={{0,32},{32,64},{64,96},{96,0},{1,33},{33,65},{65,97},{97,1},{2,34}... | collective-permute-start | bytes 1179656 | tf_op jit(solution)/shard_map/ppermute | solution.py:241
  39.3 14.9 %all-to-all-start.1 = ((bf16[8,3,32,256]{3,2,1,0:T(8,128)(2,1)}), bf16[8,3,32,256]{3,2,1,0:T(8,128)(2,1)S(1)}, u32[]{:S(2)}, u32[]{:S(2)}) async-start(bf16[8,3,32,256]{3,2,1,0:T(8,128)(2,1)} %copy-done.11), calls=%async_computation.1 | async-start | bytes 786432 | tf_op jit(solution)/shard_map/all_to_all | solution.py:300
  43.4 13.8 %collective-permute-start.2 = (bf16[3,8,32,256]{3,2,1,0:T(8,128)(2,1)S(1)}, bf16[3,8,32,256]{3,2,1,0:T(8,128)(2,1)S(1)}, u32[]{:S(2)}, u32[]{:S(2)}) collective-permute-start(bf16[3,8,32,256]{3,2,1,0:T(8,128)(2,1)S(1)} %get-tuple-element.14.refs_0_), channel_id=1, source_target_pairs={{0,96},{32,0},{64,32},{96,64},{1,97},{33,1},{65,33},{97,65},{2,98}... | collective-permute-start | bytes 1179656 | tf_op jit(solution)/shard_map/ppermute | solution.py:242
  46.1 12.7 %collective-permute-start.4 = (bf16[3,8,32,256]{3,2,1,0:T(8,128)(2,1)S(1)}, bf16[3,8,32,256]{3,2,1,0:T(8,128)(2,1)}, u32[]{:S(2)}, u32[]{:S(2)}) collective-permute-start(bf16[3,8,32,256]{3,2,1,0:T(8,128)(2,1)S(1)} %get-tuple-element.14.refs_0_), channel_id=1, source_target_pairs={{0,16},{16,0},{1,17},{17,1},{2,18},{18,2},{3,19},{19,3},{4,20},{20... | collective-permute-start | bytes 1179656 | tf_op jit(solution)/shard_map/ppermute | solution.py:297
  54.1 10.0 %collective-permute-start.16 = (bf16[8,3,32,256]{3,2,1,0:T(8,128)(2,1)S(1)}, bf16[8,3,32,256]{3,2,1,0:T(8,128)(2,1)S(1)}, u32[]{:S(2)}, u32[]{:S(2)}) collective-permute-start(bf16[8,3,32,256]{3,2,1,0:T(8,128)(2,1)S(1)} %all-to-all-done.1.refs_8_), channel_id=1, source_target_pairs={{0,2},{2,4},{4,6},{6,0},{1,3},{3,5},{5,7},{7,1},{8,10},{10,12},{12... | collective-permute-start | bytes 1179656 | tf_op jit(solution)/shard_map/ppermute | solution.py:241
  54.1 30.3 %copy-start.7 = (bf16[3,8,32,256]{3,2,1,0:T(8,128)(2,1)}, bf16[3,8,32,256]{3,2,1,0:T(8,128)(2,1)S(1)}, u32[]{:S(2)}) copy-start(bf16[3,8,32,256]{3,2,1,0:T(8,128)(2,1)S(1)} %collective-permute-done.1.refs_1_) | copy-start | bytes 1179652
  54.1 13.1 %collective-permute-start.19 = (bf16[8,3,32,256]{3,2,1,0:T(8,128)(2,1)S(1)}, bf16[8,3,32,256]{3,2,1,0:T(8,128)(2,1)S(1)}, u32[]{:S(2)}, u32[]{:S(2)}) collective-permute-start(bf16[8,3,32,256]{3,2,1,0:T(8,128)(2,1)S(1)} %all-to-all-done.1.refs_8_), channel_id=1, source_target_pairs={{0,8},{8,0},{1,9},{9,1},{2,10},{10,2},{3,11},{11,3},{4,12},{12,4},... | collective-permute-start | bytes 1179656 | tf_op jit(solution)/shard_map/ppermute | solution.py:301
  57.3 27.1 %copy-start.9 = (bf16[3,8,32,256]{3,2,1,0:T(8,128)(2,1)}, bf16[3,8,32,256]{3,2,1,0:T(8,128)(2,1)S(1)}, u32[]{:S(2)}) copy-start(bf16[3,8,32,256]{3,2,1,0:T(8,128)(2,1)S(1)} %collective-permute-done.2.refs_2_) | copy-start | bytes 1179652
  57.3 10.0 %collective-permute-start.3 = (bf16[3,8,32,256]{3,2,1,0:T(8,128)(2,1)S(1)}, bf16[3,8,32,256]{3,2,1,0:T(8,128)(2,1)S(1)}, u32[]{:S(2)}, u32[]{:S(2)}) collective-permute-start(bf16[3,8,32,256]{3,2,1,0:T(8,128)(2,1)S(1)} %collective-permute-done.1.refs_1_), channel_id=1, source_target_pairs={{0,32},{32,64},{64,96},{96,0},{1,33},{33,65},{65,97},{97,1},{2,34}... | collective-permute-start | bytes 1179656 | tf_op jit(solution)/shard_map/ppermute | solution.py:243
  58.8 11.4 %collective-permute-start.6 = (bf16[3,8,32,256]{3,2,1,0:T(8,128)(2,1)}, bf16[3,8,32,256]{3,2,1,0:T(8,128)(2,1)S(1)}, u32[]{:S(2)}, u32[]{:S(2)}) collective-permute-start(bf16[3,8,32,256]{3,2,1,0:T(8,128)(2,1)} %collective-permute-done.4.refs_4_), channel_id=1, source_target_pairs={{0,96},{32,0},{64,32},{96,64},{1,97},{33,1},{65,33},{97,65},{2,98}... | collective-permute-start | bytes 1179656 | tf_op jit(solution)/shard_map/ppermute | solution.py:242
  64.2 12.1 %collective-permute-start.5 = (bf16[3,8,32,256]{3,2,1,0:T(8,128)(2,1)}, bf16[3,8,32,256]{3,2,1,0:T(8,128)(2,1)S(1)}, u32[]{:S(2)}, u32[]{:S(2)}) collective-permute-start(bf16[3,8,32,256]{3,2,1,0:T(8,128)(2,1)} %collective-permute-done.4.refs_4_), channel_id=1, source_target_pairs={{0,32},{32,64},{64,96},{96,0},{1,33},{33,65},{65,97},{97,1},{2,34}... | collective-permute-start | bytes 1179656 | tf_op jit(solution)/shard_map/ppermute | solution.py:241
  67.3 8.9 %collective-permute-start.21 = (bf16[8,3,32,256]{3,2,1,0:T(8,128)(2,1)S(1)}, bf16[8,3,32,256]{3,2,1,0:T(8,128)(2,1)S(1)}, u32[]{:S(2)}, u32[]{:S(2)}) collective-permute-start(bf16[8,3,32,256]{3,2,1,0:T(8,128)(2,1)S(1)} %collective-permute-done.19.refs_12_), channel_id=1, source_target_pairs={{0,6},{2,0},{4,2},{6,4},{1,7},{3,1},{5,3},{7,5},{8,14},{10,8},{12,... | collective-permute-start | bytes 1179656 | tf_op jit(solution)/shard_map/ppermute | solution.py:242
  67.3 27.3 %collective-permute-start.17 = (bf16[8,3,32,256]{3,2,1,0:T(8,128)(2,1)S(1)}, bf16[8,3,32,256]{3,2,1,0:T(8,128)(2,1)S(1)}, u32[]{:S(2)}, u32[]{:S(2)}) collective-permute-start(bf16[8,3,32,256]{3,2,1,0:T(8,128)(2,1)S(1)} %all-to-all-done.1.refs_8_), channel_id=1, source_target_pairs={{0,6},{2,0},{4,2},{6,4},{1,7},{3,1},{5,3},{7,5},{8,14},{10,8},{12,... | collective-permute-start | bytes 1179656 | tf_op jit(solution)/shard_map/ppermute | solution.py:242
  70.2 14.2 %collective-permute-start.7 = (bf16[3,8,32,256]{3,2,1,0:T(8,128)(2,1)S(1)}, bf16[3,8,32,256]{3,2,1,0:T(8,128)(2,1)S(1)}, u32[]{:S(2)}, u32[]{:S(2)}) collective-permute-start(bf16[3,8,32,256]{3,2,1,0:T(8,128)(2,1)S(1)} %collective-permute-done.6.refs_6_), channel_id=1, source_target_pairs={{0,96},{32,0},{64,32},{96,64},{1,97},{33,1},{65,33},{97,65},{2,98}... | collective-permute-start | bytes 1179656 | tf_op jit(solution)/shard_map/ppermute | solution.py:243
  76.2 18.4 %collective-permute-start.20 = (bf16[8,3,32,256]{3,2,1,0:T(8,128)(2,1)S(1)}, bf16[8,3,32,256]{3,2,1,0:T(8,128)(2,1)S(1)}, u32[]{:S(2)}, u32[]{:S(2)}) collective-permute-start(bf16[8,3,32,256]{3,2,1,0:T(8,128)(2,1)S(1)} %collective-permute-done.19.refs_12_), channel_id=1, source_target_pairs={{0,2},{2,4},{4,6},{6,0},{1,3},{3,5},{5,7},{7,1},{8,10},{10,12},{12... | collective-permute-start | bytes 1179656 | tf_op jit(solution)/shard_map/ppermute | solution.py:241
  76.2 18.4 %collective-permute-start.18 = (bf16[8,3,32,256]{3,2,1,0:T(8,128)(2,1)S(1)}, bf16[8,3,32,256]{3,2,1,0:T(8,128)(2,1)S(1)}, u32[]{:S(2)}, u32[]{:S(2)}) collective-permute-start(bf16[8,3,32,256]{3,2,1,0:T(8,128)(2,1)S(1)} %collective-permute-done.16.refs_9_), channel_id=1, source_target_pairs={{0,2},{2,4},{4,6},{6,0},{1,3},{3,5},{5,7},{7,1},{8,10},{10,12},{12... | collective-permute-start | bytes 1179656 | tf_op jit(solution)/shard_map/ppermute | solution.py:243
  77.8 16.9 %collective-permute-start.22 = (bf16[8,3,32,256]{3,2,1,0:T(8,128)(2,1)S(1)}, bf16[8,3,32,256]{3,2,1,0:T(8,128)(2,1)S(1)}, u32[]{:S(2)}, u32[]{:S(2)}) collective-permute-start(bf16[8,3,32,256]{3,2,1,0:T(8,128)(2,1)S(1)} %collective-permute-done.21.refs_14_), channel_id=1, source_target_pairs={{0,6},{2,0},{4,2},{6,4},{1,7},{3,1},{5,3},{7,5},{8,14},{10,8},{12,... | collective-permute-start | bytes 1179656 | tf_op jit(solution)/shard_map/ppermute | solution.py:243
  79.2 2.2 %copy-start.1 = (bf16[2048,1024]{1,0:T(8,128)(2,1)S(1)}, bf16[2048,1024]{1,0:T(8,128)(2,1)}, u32[]{:S(2)}) copy-start(bf16[2048,1024]{1,0:T(8,128)(2,1)} %own_ref.1) | copy-start | bytes 12582916
  84.4 1.0 copy-start.8
  85.4 1.0 copy-start.10
  94.5 4.8 %copy-start.3 = (s16[272,768]{1,0:T(8,128)(2,1)}, s16[272,768]{1,0:T(8,128)(2,1)S(1)}, u32[]{:S(2)}) copy-start(s16[272,768]{1,0:T(8,128)(2,1)S(1)} %get-tuple-element.21.refs_1_) | copy-start | bytes 1253380
  94.6 4.8 %copy-start.4 = (s16[272,768]{1,0:T(8,128)(2,1)}, s16[272,768]{1,0:T(8,128)(2,1)S(1)}, u32[]{:S(2)}) copy-start(s16[272,768]{1,0:T(8,128)(2,1)S(1)} %get-tuple-element.20.refs_4_) | copy-start | bytes 1253380
  94.6 4.8 %copy-start.5 = (s16[272,768]{1,0:T(8,128)(2,1)}, s16[272,768]{1,0:T(8,128)(2,1)S(1)}, u32[]{:S(2)}) copy-start(s16[272,768]{1,0:T(8,128)(2,1)S(1)} %get-tuple-element.19.refs_2_) | copy-start | bytes 1253380
  94.6 4.8 %copy-start.6 = (s16[272,768]{1,0:T(8,128)(2,1)}, s16[272,768]{1,0:T(8,128)(2,1)S(1)}, u32[]{:S(2)}) copy-start(s16[272,768]{1,0:T(8,128)(2,1)S(1)} %get-tuple-element.18.refs_7_) | copy-start | bytes 1253380
  99.4 24.5 %all-to-all-start.2 = ((s16[64,8,512]{2,1,0:T(8,128)(2,1)}), s16[64,8,512]{2,1,0:T(8,128)(2,1)S(1)}, u32[]{:S(2)}, u32[]{:S(2)}) async-start(s16[64,8,512]{2,1,0:T(8,128)(2,1)} %bitcast.9), calls=%async_computation.2 | async-start | bytes 1048576 | tf_op jit(solution)/shard_map/all_to_all | solution.py:376
  112.1 42.0 %collective-permute-start.8 = (s16[272,768]{1,0:T(8,128)(2,1)}, s16[272,768]{1,0:T(8,128)(2,1)}, u32[]{:S(2)}, u32[]{:S(2)}) collective-permute-start(s16[272,768]{1,0:T(8,128)(2,1)} %get-tuple-element.16.refs_6_), channel_id=1, source_target_pairs={{0,12},{2,14},{4,8},{6,10},{8,4},{10,6},{12,0},{14,2},{1,13},{3,15... | collective-permute-start | bytes 1253384 | tf_op jit(solution)/shard_map/ppermute | solution.py:357
  117.1 37.5 %collective-permute-start.9 = (s16[272,768]{1,0:T(8,128)(2,1)}, s16[272,768]{1,0:T(8,128)(2,1)}, u32[]{:S(2)}, u32[]{:S(2)}) collective-permute-start(s16[272,768]{1,0:T(8,128)(2,1)} %get-tuple-element.17.refs_5_), channel_id=1, source_target_pairs={{0,10},{2,12},{4,14},{6,8},{8,2},{10,4},{12,6},{14,0},{1,11},{3,13... | collective-permute-start | bytes 1253384 | tf_op jit(solution)/shard_map/ppermute | solution.py:357
  124.2 1.0 copy-start.2
  125.2 71.2 %all-to-all-start.3 = ((s16[128,8,512]{2,1,0:T(8,128)(2,1)}), s16[128,8,512]{2,1,0:T(8,128)(2,1)S(1)}, u32[]{:S(2)}, u32[]{:S(2)}) async-start(s16[128,8,512]{2,1,0:T(8,128)(2,1)} %copy-done.2), calls=%async_computation.3 | async-start | bytes 2097152 | tf_op jit(solution)/shard_map/all_to_all | solution.py:393
  147.8 25.5 %collective-permute-start.10 = (s16[272,768]{1,0:T(8,128)(2,1)}, s16[272,768]{1,0:T(8,128)(2,1)S(1)}, u32[]{:S(2)}, u32[]{:S(2)}) collective-permute-start(s16[272,768]{1,0:T(8,128)(2,1)} %copy-done.6), channel_id=1, source_target_pairs={{0,14},{2,8},{4,10},{6,12},{8,6},{10,0},{12,2},{14,4},{1,15},{3,9}... | collective-permute-start | bytes 1253384 | tf_op jit(solution)/shard_map/ppermute | solution.py:357
  153.5 19.9 %collective-permute-start.11 = (s16[272,768]{1,0:T(8,128)(2,1)}, s16[272,768]{1,0:T(8,128)(2,1)S(1)}, u32[]{:S(2)}, u32[]{:S(2)}) collective-permute-start(s16[272,768]{1,0:T(8,128)(2,1)} %copy-done.5), channel_id=1, source_target_pairs={{0,4},{2,6},{4,0},{6,2},{8,12},{10,14},{12,8},{14,10},{1,5},{3,7},... | collective-permute-start | bytes 1253384 | tf_op jit(solution)/shard_map/ppermute | solution.py:357
  153.9 28.8 %collective-permute-start.12 = (s16[272,768]{1,0:T(8,128)(2,1)}, s16[272,768]{1,0:T(8,128)(2,1)S(1)}, u32[]{:S(2)}, u32[]{:S(2)}) collective-permute-start(s16[272,768]{1,0:T(8,128)(2,1)} %copy-done.4), channel_id=1, source_target_pairs={{0,8},{2,10},{4,12},{6,14},{8,0},{10,2},{12,4},{14,6},{1,9},{3,11}... | collective-permute-start | bytes 1253384 | tf_op jit(solution)/shard_map/ppermute | solution.py:357
  154.1 28.7 %collective-permute-start.13 = (s16[272,768]{1,0:T(8,128)(2,1)}, s16[272,768]{1,0:T(8,128)(2,1)S(1)}, u32[]{:S(2)}, u32[]{:S(2)}) collective-permute-start(s16[272,768]{1,0:T(8,128)(2,1)} %copy-done.3), channel_id=1, source_target_pairs={{0,2},{2,4},{4,6},{6,0},{8,10},{10,12},{12,14},{14,8},{1,3},{3,5},... | collective-permute-start | bytes 1253384 | tf_op jit(solution)/shard_map/ppermute | solution.py:357
  154.6 34.3 %collective-permute-start.14 = (s16[272,768]{1,0:T(8,128)(2,1)S(1)}, s16[272,768]{1,0:T(8,128)(2,1)S(1)}, u32[]{:S(2)}, u32[]{:S(2)}) collective-permute-start(s16[272,768]{1,0:T(8,128)(2,1)S(1)} %get-tuple-element.22.refs_3_), channel_id=1, source_target_pairs={{0,6},{2,0},{4,2},{6,4},{8,14},{10,8},{12,10},{14,12},{1,7},{3,1},... | collective-permute-start | bytes 1253384 | tf_op jit(solution)/shard_map/ppermute | solution.py:357
  191.6 0.7 copy-start.12
  192.3 2.2 %collective-permute-start.15 = (bf16[128,768]{1,0:T(8,128)(2,1)}, bf16[128,768]{1,0:T(8,128)(2,1)S(1)}, u32[]{:S(2)}, u32[]{:S(2)}) collective-permute-start(bf16[128,768]{1,0:T(8,128)(2,1)} %get-tuple-element.24), channel_id=1, source_target_pairs={{0,1},{1,0},{2,3},{3,2},{4,5},{5,4},{6,7},{7,6},{8,9},{9,8},{10,11... | collective-permute-start | bytes 589832 | tf_op jit(solution)/shard_map/ppermute | solution.py:368
where the time goes:
time: 199 us; the launch traced here: 198 us
  waiting for transfers between devices  83.4 us (42%)
  starting transfers between devices  80.4 us (40%)
  Pallas kernels  23.9 us (12%)
  local copies, waits for them, and re-layouts  7.21 us (4%)
  other arithmetic  1.99 us (1%)
    ppermute x7, waiting for transfers between devices, update(): sums.append(lax.ppermute(coded[j], HY, to))  32.1 us
    all_to_all x1, waiting for transfers between devices, update(): lax.all_to_all(share, ('h', 'y', 'c'), split_axis=0, concat_axis=0, tiled...  22.7 us
    all_to_all x1, starting transfers between devices, update(): lax.all_to_all(piece, CHIPS + ('c',), split_axis=0, concat_axis=0, tiled=...  22.6 us
    ppermute x7, starting transfers between devices, update(): sums.append(lax.ppermute(coded[j], HY, to))  14.2 us
    all_to_all x1, starting transfers between devices, update(): diag = lax.all_to_all(diag, CHIPS, split_axis=0, concat_axis=0, tiled=True)  12.7 us
    ppermute x4, waiting for transfers between devices, spread(): below = lax.ppermute(own, axis, UP)  8.75 us
    pallas_call x1, Pallas kernels, update(): pl.pallas_call(product_kernel, out_shape=[jax.ShapeDtypeStruct((size + 16...  8.1 us
    all_to_all x1, starting transfers between devices, update(): lax.all_to_all(share, ('h', 'y', 'c'), split_axis=0, concat_axis=0, tiled...  8.03 us
  transfers between devices with their start and end apart: 27, of which 13 were waited for; matrix products, arithmetic and copies ran while one was open for 1% of the time, Pallas kernels for 9%

commit v1 on v0

--- a/solution.py
+++ b/solution.py
@@ -12,7 +12,6 @@
 NX, NL, NH, NY, NC = 4, 2, 2, 4, 2
 XL = ("x", "l")
 HY = ("h", "y")
-CHIPS = XL + HY
 CORE_SWAP = [(0, 1), (1, 0)]
 UP = [(i, (i + 1) % NX) for i in range(NX)]
 DOWN = [(i, (i - 1) % NX) for i in range(NX)]
@@ -202,23 +201,29 @@
         swap_ref[:, cols] = jnp.where(first, rounded[slab:], rounded[:slab])
 
 
-def piece_kernel(q_ref, inverse_ref, o_ref):
+def sum_of(q_ref):
     width = q_ref.shape[2] - LANES
     scale = scale_of(plain(q_ref[:, :, width:]))
     sums = [
         jnp.sum(plain(q_ref[:, :, i : i + LANES]) * scale, axis=0) for i in range(0, width, LANES)
     ]
-    values = inverse_ref[...] - jnp.concatenate(sums, axis=1)
+    return jnp.concatenate(sums, axis=1)
+
+
+def send(o_ref, values):
     level = level_of(jnp.max(jnp.abs(values), keepdims=True))
-    coded = jnp.concatenate(
-        [
-            code(values, level),
-            jnp.broadcast_to(level, (values.shape[0], LANES)).astype(jnp.int32).astype(I16),
-        ],
-        axis=1,
-    )
+    tail = jnp.broadcast_to(level, (values.shape[0], LANES)).astype(jnp.int32).astype(I16)
+    coded = jnp.concatenate([code(values, level), tail], axis=1)
     for j in range(o_ref.shape[0]):
         o_ref[j] = coded
+
+
+def partial_kernel(q_ref, o_ref):
+    send(o_ref, sum_of(q_ref))
+
+
+def piece_kernel(q_ref, inverse_ref, o_ref):
+    send(o_ref, inverse_ref[...] - sum_of(q_ref))
 
 
 def total_kernel(q_ref, o_ref):
@@ -227,14 +232,16 @@
     width = reach - LANES
     count = pieces // 2
     for c in range(cores):
-        for i in range(2):
-            rows = slice(i * count, (i + 1) * count)
-            scale = scale_of(plain(q_ref[rows, c, :, width:]))
+        for g in range(pieces):
+            rows = slice(g % count * depth, (g % count + 1) * depth)
+            scale = scale_of(plain(q_ref[g, c, :, width:]))
             for t in range(width // LANES):
-                lane = (i * width + t * LANES) % size
-                k = c * (supers // cores) + (i * width + t * LANES) // size
-                values = plain(q_ref[rows, c, :, t * LANES : (t + 1) * LANES]) * scale
-                o_ref[k, :, lane : lane + LANES] = values.reshape(count * depth, LANES)
+                column = g // count * width + t * LANES
+                k = c * (supers // cores) + column // size
+                lane = column % size
+                o_ref[k, rows, lane : lane + LANES] = (
+                    plain(q_ref[g, c, :, t * LANES : (t + 1) * LANES]) * scale
+                )
 
 
 def spread(own, axis, up):
@@ -333,8 +340,7 @@
         compiler_params=pltpu.CompilerParams(vmem_limit_bytes=20 << 20),
         name="product",
     )(place, where, staged, *window_parts)
-    pieces = groups * chips
-    depth = 2 * size // pieces
+    depth = 2 * size // groups
     reach = width // 2 + LANES
     diag = pl.pallas_call(
         diagonal_kernel,
@@ -372,25 +378,34 @@
         jnp.concatenate([theirs, mine], axis=1),
     )
 
-    diag = diag.reshape(pieces, depth, reach)
-    diag = lax.all_to_all(diag, CHIPS, split_axis=0, concat_axis=0, tiled=True)
-    index = group * chips + chip
+    small = pltpu.CompilerParams(vmem_limit_bytes=6 << 20)
+    diag = diag.reshape(groups, depth, reach)
+    diag = lax.all_to_all(diag, XL, split_axis=0, concat_axis=0, tiled=True)
+    diag = pl.pallas_call(
+        partial_kernel,
+        out_shape=jax.ShapeDtypeStruct((chips, depth, reach), I16),
+        in_specs=[vmem],
+        out_specs=vmem,
+        compiler_params=small,
+        name="partial",
+    )(diag)
+    diag = lax.all_to_all(diag, HY, split_axis=0, concat_axis=0, tiled=True)
     inverse = lax.dynamic_slice(
         diag_inverse,
-        (core * members, index % (pieces // 2) * depth, 0),
+        (core * members, group % (groups // 2) * depth, 0),
         (members, depth, size),
     )
     inverse = jnp.transpose(inverse, (1, 0, 2)).reshape(depth, 2, width // 2)
-    inverse = lax.dynamic_index_in_dim(inverse, index // (pieces // 2), 1, keepdims=False)
+    inverse = lax.dynamic_index_in_dim(inverse, group // (groups // 2), 1, keepdims=False)
     piece = pl.pallas_call(
         piece_kernel,
-        out_shape=jax.ShapeDtypeStruct((pieces * NC, depth, reach), I16),
+        out_shape=jax.ShapeDtypeStruct((groups * NC, depth, reach), I16),
         in_specs=[vmem, vmem],
         out_specs=vmem,
-        compiler_params=pltpu.CompilerParams(vmem_limit_bytes=6 << 20),
+        compiler_params=pltpu.CompilerParams(vmem_limit_bytes=60 << 20),
         name="piece",
     )(diag, inverse)
-    whole = lax.all_to_all(piece, CHIPS + ("c",), split_axis=0, concat_axis=0, tiled=True)
+    whole = lax.all_to_all(piece, XL + ("c",), split_axis=0, concat_axis=0, tiled=True)
     diagonal = pl.pallas_call(
         total_kernel,
         out_shape=jax.ShapeDtypeStruct(diag_inverse.shape, F32),
@@ -398,7 +413,7 @@
         out_specs=vmem,
         compiler_params=pltpu.CompilerParams(vmem_limit_bytes=12 << 20),
         name="total",
-    )(whole.reshape(pieces, NC, depth, reach))
+    )(whole.reshape(groups, NC, depth, reach))
     return column_block, diagonal
 
 

time: 199 us -> 197 us (0.990)
  starting transfers between devices: 80.4 us -> 63.4 us
  blocking collectives: 0 us -> 15.1 us
  waiting for transfers between devices: 83.4 us -> 81 us
  Pallas kernels: 23.9 us -> 26.1 us
    all_to_all x2, starting transfers between devices: 35.3 us -> 20.1 us  [the longest x1 12.2 us: update(): lax.all_to_all(piece, XL + ('c',), split_axis=0, concat_axis=0, tiled=True)]
    all_to_all x0 -> x1, blocking collectives: none -> 15.1 us  [update(): diag = lax.all_to_all(diag, XL, split_axis=0, concat_axis=0, tiled=True)]
    pallas_call x1 -> x2, Pallas kernels: 0.37 us -> 3.56 us  [the longest x1 2.41 us: update(): pl.pallas_call(piece_kernel, out_shape=jax.ShapeDtypeStruct((groups * NC,...]
    unnamed x32 -> x33, local copies, waits for them, and re-layouts: 6.6 us -> 7.08 us
  transfers between devices with their start and end apart: 27 -> 27, of which waited for: 13 -> 13; matrix products, arithmetic and copies ran while one was open for 1% -> 2% of each run, Pallas kernels for 9% -> 10%
where the time goes in v1:
time: 197 us
  waiting for transfers between devices  81 us (41%)
  starting transfers between devices  63.4 us (32%)
  Pallas kernels  26.1 us (13%)
  blocking collectives  15.1 us (8%)
  local copies, waits for them, and re-layouts  8.12 us (4%)
  other arithmetic  1.99 us (1%)
    ppermute x7, waiting for transfers between devices, update(): sums.append(lax.ppermute(coded[j], HY, to))  31 us
    all_to_all x1, waiting for transfers between devices, update(): lax.all_to_all(share, ('h', 'y', 'c'), split_axis=0, concat_axis=0, tiled...  22.7 us
    all_to_all x1, blocking collectives, update(): diag = lax.all_to_all(diag, XL, split_axis=0, concat_axis=0, tiled=True)  15.1 us
    ppermute x7, starting transfers between devices, update(): sums.append(lax.ppermute(coded[j], HY, to))  12.3 us
    all_to_all x1, starting transfers between devices, update(): lax.all_to_all(piece, XL + ('c',), split_axis=0, concat_axis=0, tiled=True)  12.2 us
    ppermute x4, waiting for transfers between devices, spread(): below = lax.ppermute(own, axis, UP)  8.75 us
    pallas_call x1, Pallas kernels, update(): pl.pallas_call(product_kernel, out_shape=[jax.ShapeDtypeStruct((size + 16...  8.04 us
    all_to_all x1, starting transfers between devices, update(): lax.all_to_all(share, ('h', 'y', 'c'), split_axis=0, concat_axis=0, tiled...  8.03 us
  transfers between devices with their start and end apart: 27, of which 13 were waited for; matrix products, arithmetic and copies ran while one was open for 2% of the time, Pallas kernels for 10%

profile of v1, /device:TPU:1, one launch (start us, length us, event | category | flops | bytes accessed | tf_op | source)
XLA Modules:
  0.0 196.7 jit_solution(3088296162067594013)
XLA Ops:
  0.6 1.5 collective-permute-start
  2.7 2.8 %share.1 = bf16[16,2,3,32,256]{4,3,2,1,0:T(8,128)(2,1)} custom-call(s32[7]{0:T(128)} %stack.31.where, bf16[2,6,256,256]{3,2,1,0:T(8,128)(2,1)} %bitcast.19), custom_call_target="tpu_custom_call" | custom-call | tf_op jit(solution)/shard_map/share/pallas_call | solution.py:281
  5.6 8.0 %all-to-all-start = ((bf16[16,2,3,32,256]{4,3,2,1,0:T(8,128)(2,1)}), bf16[16,2,3,32,256]{4,3,2,1,0:T(8,128)(2,1)S(1)}, u32[]{:S(2)}, u32[]{:S(2)}) async-start(bf16[16,2,3,32,256]{4,3,2,1,0:T(8,128)(2,1)} %share.1), calls=%async_computation | async-start | bytes 3145728 | tf_op jit(solution)/shard_map/all_to_all | solution.py:292
  13.8 22.7 %all-to-all-done = bf16[16,2,3,32,256]{4,3,2,1,0:T(8,128)(2,1)S(1)} async-done(((bf16[16,2,3,32,256]{4,3,2,1,0:T(8,128)(2,1)}), bf16[16,2,3,32,256]{4,3,2,1,0:T(8,128)(2,1)S(1)}, u32[]{:S(2)}, u32[]{:S(2)}) %all-to-all-start) | async-done | bytes 1572896 | tf_op jit(solution)/shard_map/all_to_all | solution.py:292
  36.5 0.8 pick.1
  37.3 0.7 copy-done.10
  38.0 1.2 collective-permute-start.1
  39.3 4.2 %all-to-all-start.1 = ((bf16[8,3,32,256]{3,2,1,0:T(8,128)(2,1)}), bf16[8,3,32,256]{3,2,1,0:T(8,128)(2,1)S(1)}, u32[]{:S(2)}, u32[]{:S(2)}) async-start(bf16[8,3,32,256]{3,2,1,0:T(8,128)(2,1)} %copy-done.10), calls=%async_computation.1 | async-start | bytes 786432 | tf_op jit(solution)/shard_map/all_to_all | solution.py:307
  43.4 2.7 %collective-permute-start.2 = (bf16[3,8,32,256]{3,2,1,0:T(8,128)(2,1)S(1)}, bf16[3,8,32,256]{3,2,1,0:T(8,128)(2,1)S(1)}, u32[]{:S(2)}, u32[]{:S(2)}) collective-permute-start(bf16[3,8,32,256]{3,2,1,0:T(8,128)(2,1)S(1)} %get-tuple-element.14.refs_0_), channel_id=1, source_target_pairs={{0,96},{32,0},{64,32},{96,64},{1,97},{33,1},{65,33},{97,65},{2,98}... | collective-permute-start | bytes 1179656 | tf_op jit(solution)/shard_map/ppermute | solution.py:249
  46.1 1.2 collective-permute-start.4
  47.3 6.8 %all-to-all-done.1.refs_8_ = bf16[8,3,32,256]{3,2,1,0:T(8,128)(2,1)S(1)} async-done(((bf16[8,3,32,256]{3,2,1,0:T(8,128)(2,1)}), bf16[8,3,32,256]{3,2,1,0:T(8,128)(2,1)S(1)}, u32[]{:S(2)}, u32[]{:S(2)}) %all-to-all-start.1) | async-done | bytes 393248 | tf_op jit(solution)/shard_map/all_to_all | solution.py:307
  54.1 1.4 collective-permute-start.19
  55.6 1.7 collective-permute-done.2.refs_2_
  57.3 1.2 collective-permute-start.3
  58.8 1.9 collective-permute-start.6
  60.7 3.4 %collective-permute-done.16.refs_9_ = bf16[8,3,32,256]{3,2,1,0:T(8,128)(2,1)S(1)} collective-permute-done((bf16[8,3,32,256]{3,2,1,0:T(8,128)(2,1)S(1)}, bf16[8,3,32,256]{3,2,1,0:T(8,128)(2,1)S(1)}, u32[]{:S(2)}, u32[]{:S(2)}) %collective-permute-start.16) | collective-permute-done | bytes 393248 | tf_op jit(solution)/shard_map/ppermute | solution.py:248
  64.2 3.1 %collective-permute-done.19.refs_12_ = bf16[8,3,32,256]{3,2,1,0:T(8,128)(2,1)S(1)} collective-permute-done((bf16[8,3,32,256]{3,2,1,0:T(8,128)(2,1)S(1)}, bf16[8,3,32,256]{3,2,1,0:T(8,128)(2,1)S(1)}, u32[]{:S(2)}, u32[]{:S(2)}) %collective-permute-start.19) | collective-permute-done | bytes 393248 | tf_op jit(solution)/shard_map/ppermute | solution.py:308
  67.3 2.9 %collective-permute-start.17 = (bf16[8,3,32,256]{3,2,1,0:T(8,128)(2,1)S(1)}, bf16[8,3,32,256]{3,2,1,0:T(8,128)(2,1)S(1)}, u32[]{:S(2)}, u32[]{:S(2)}) collective-permute-start(bf16[8,3,32,256]{3,2,1,0:T(8,128)(2,1)S(1)} %all-to-all-done.1.refs_8_), channel_id=1, source_target_pairs={{0,6},{2,0},{4,2},{6,4},{1,7},{3,1},{5,3},{7,5},{8,14},{10,8},{12,... | collective-permute-start | bytes 1179656 | tf_op jit(solution)/shard_map/ppermute | solution.py:249
  70.2 0.7 collective-permute-start.7
  70.9 5.3 %collective-permute-done.5.refs_5_ = bf16[3,8,32,256]{3,2,1,0:T(8,128)(2,1)S(1)} collective-permute-done((bf16[3,8,32,256]{3,2,1,0:T(8,128)(2,1)}, bf16[3,8,32,256]{3,2,1,0:T(8,128)(2,1)S(1)}, u32[]{:S(2)}, u32[]{:S(2)}) %collective-permute-start.5) | collective-permute-done | bytes 393248 | tf_op jit(solution)/shard_map/ppermute | solution.py:248
  76.2 1.6 collective-permute-start.18
  77.8 1.3 collective-permute-start.22
  79.2 2.2 %copy-done.1 = bf16[2048,1024]{1,0:T(8,128)(2,1)S(1)} copy-done((bf16[2048,1024]{1,0:T(8,128)(2,1)S(1)}, bf16[2048,1024]{1,0:T(8,128)(2,1)}, u32[]{:S(2)}) %copy-start.1) | copy-done | bytes 4194328
  81.4 3.0 %stage.1.a_ref = bf16[2,2048,1024]{2,1,0:T(8,128)(2,1)S(1)} custom-call(s32[7]{0:T(128)S(1)} %copy-done.12, bf16[2048,1024]{1,0:T(8,128)(2,1)S(1)} %copy-done.1, bf16[2048,1024]{1,0:T(8,128)(2,1)} %collective-permute-done.other_ref), custom_call_target="tpu_custom_call" | custom-call | tf_op jit(solution)/shard_map/stage/pallas_call | solution.py:312
  84.4 1.0 copy-done.7
  85.4 1.0 copy-done.9
  86.4 8.0 %product.1 = (s16[272,768]{1,0:T(8,128)(2,1)S(1)}, s16[272,768]{1,0:T(8,128)(2,1)S(1)}, s16[272,768]{1,0:T(8,128)(2,1)S(1)}, s16[272,768]{1,0:T(8,128)(2,1)S(1)}...) custom-call(s32[6,64]{1,0:T(8,128)S(1)} %select_reduce_fusion.place,, ...), custom_call_target="tpu_custom_call" | custom-call | tf_op jit(solution)/shard_map/product/pallas_call | solution.py:325
  94.7 3.8 %diagonal.1 = s16[2,256,512]{2,1,0:T(8,128)(2,1)S(1)} custom-call(s32[6,64]{1,0:T(8,128)S(1)} %select_reduce_fusion.place, s32[7]{0:T(128)S(1)} %copy-done.12, s16[272,768]{1,0:T(8,128)(2,1)S(1)} %get-tuple-element.15.refs_0_, s16[272,768]{1,0:T(8,128)(2,1)S(1)} %get-tuple-element.21.refs_1_, s16[272,768]{1,0:T(8,128)(2,1)S(1)} %get-tuple-element.19.refs_2_, ...), custom_call_target="tpu_custom_call" | custom-call | tf_op jit(solution)/shard_map/diagonal/pallas_call | solution.py:345
  98.5 15.1 %all_to_all.25.q_ref = s16[8,64,512]{2,1,0:T(8,128)(2,1)S(1)} all-to-all(s16[8,64,512]{2,1,0:T(8,128)(2,1)S(1)} %bitcast.18), channel_id=1, replica_groups=mesh['x'=4,'l'=2,'h'=2,'y'=4,'c'=2] {'x','l'}, dimensions={0} | all-to-all | bytes 1048576 | tf_op jit(solution)/shard_map/all_to_all | solution.py:383
  113.6 1.2 partial.1
  114.8 8.0 %all-to-all-start.3 = ((s16[8,64,512]{2,1,0:T(8,128)(2,1)}), s16[8,64,512]{2,1,0:T(8,128)(2,1)S(1)}, u32[]{:S(2)}, u32[]{:S(2)}) async-start(s16[8,64,512]{2,1,0:T(8,128)(2,1)} %partial.1), calls=%async_computation.3 | async-start | bytes 1048576 | tf_op jit(solution)/shard_map/all_to_all | solution.py:392
  122.7 5.4 %collective-permute-start.8 = (s16[272,768]{1,0:T(8,128)(2,1)}, s16[272,768]{1,0:T(8,128)(2,1)}, u32[]{:S(2)}, u32[]{:S(2)}) collective-permute-start(s16[272,768]{1,0:T(8,128)(2,1)} %get-tuple-element.16.refs_6_), channel_id=1, source_target_pairs={{0,12},{2,14},{4,8},{6,10},{8,4},{10,6},{12,0},{14,2},{1,13},{3,15... | collective-permute-start | bytes 1253384 | tf_op jit(solution)/shard_map/ppermute | solution.py:363
  129.5 5.2 %all-to-all-done.3.q_ref = s16[8,64,512]{2,1,0:T(8,128)(2,1)S(1)} async-done(((s16[8,64,512]{2,1,0:T(8,128)(2,1)}), s16[8,64,512]{2,1,0:T(8,128)(2,1)S(1)}, u32[]{:S(2)}, u32[]{:S(2)}) %all-to-all-start.3) | async-done | bytes 524320 | tf_op jit(solution)/shard_map/all_to_all | solution.py:392
  134.7 0.8 copy-done.13
  135.5 2.4 %piece.1 = s16[16,64,512]{2,1,0:T(8,128)(2,1)} custom-call(s16[8,64,512]{2,1,0:T(8,128)(2,1)} %copy-done.13, f32[64,384]{1,0:T(8,128)} %bitcast.20), custom_call_target="tpu_custom_call" | custom-call | tf_op jit(solution)/shard_map/piece/pallas_call | solution.py:400
  137.9 12.2 %all-to-all-start.4 = ((s16[16,64,512]{2,1,0:T(8,128)(2,1)}), s16[16,64,512]{2,1,0:T(8,128)(2,1)S(1)}, u32[]{:S(2)}, u32[]{:S(2)}) async-start(s16[16,64,512]{2,1,0:T(8,128)(2,1)} %piece.1), calls=%async_computation.4 | async-start | bytes 2097152 | tf_op jit(solution)/shard_map/all_to_all | solution.py:408
  150.1 0.9 collective-permute-start.11
  151.3 3.2 %collective-permute-start.13 = (s16[272,768]{1,0:T(8,128)(2,1)}, s16[272,768]{1,0:T(8,128)(2,1)S(1)}, u32[]{:S(2)}, u32[]{:S(2)}) collective-permute-start(s16[272,768]{1,0:T(8,128)(2,1)} %copy-done.2), channel_id=1, source_target_pairs={{0,2},{2,4},{4,6},{6,0},{8,10},{10,12},{12,14},{14,8},{1,3},{3,5},... | collective-permute-start | bytes 1253384 | tf_op jit(solution)/shard_map/ppermute | solution.py:363
  154.5 2.2 %collective-permute-start.14 = (s16[272,768]{1,0:T(8,128)(2,1)S(1)}, s16[272,768]{1,0:T(8,128)(2,1)S(1)}, u32[]{:S(2)}, u32[]{:S(2)}) collective-permute-start(s16[272,768]{1,0:T(8,128)(2,1)S(1)} %get-tuple-element.22.refs_3_), channel_id=1, source_target_pairs={{0,6},{2,0},{4,2},{6,4},{8,14},{10,8},{12,10},{14,12},{1,7},{3,1},... | collective-permute-start | bytes 1253384 | tf_op jit(solution)/shard_map/ppermute | solution.py:363
  156.7 15.2 %collective-permute-done.10.refs_3_ = s16[272,768]{1,0:T(8,128)(2,1)S(1)} collective-permute-done((s16[272,768]{1,0:T(8,128)(2,1)}, s16[272,768]{1,0:T(8,128)(2,1)S(1)}, u32[]{:S(2)}, u32[]{:S(2)}) %collective-permute-start.10) | collective-permute-done | bytes 417824 | tf_op jit(solution)/shard_map/ppermute | solution.py:363
  171.9 10.0 %collective-permute-done.12.refs_5_ = s16[272,768]{1,0:T(8,128)(2,1)S(1)} collective-permute-done((s16[272,768]{1,0:T(8,128)(2,1)}, s16[272,768]{1,0:T(8,128)(2,1)S(1)}, u32[]{:S(2)}, u32[]{:S(2)}) %collective-permute-start.12) | collective-permute-done | bytes 417824 | tf_op jit(solution)/shard_map/ppermute | solution.py:363
  181.9 5.7 %collective-permute-done.14.refs_7_ = s16[272,768]{1,0:T(8,128)(2,1)S(1)} collective-permute-done((s16[272,768]{1,0:T(8,128)(2,1)S(1)}, s16[272,768]{1,0:T(8,128)(2,1)S(1)}, u32[]{:S(2)}, u32[]{:S(2)}) %collective-permute-start.14) | collective-permute-done | bytes 417824 | tf_op jit(solution)/shard_map/ppermute | solution.py:363
  187.7 2.7 %finish.1 = (bf16[128,768]{1,0:T(8,128)(2,1)S(1)}, bf16[128,768]{1,0:T(8,128)(2,1)}) custom-call(s32[6,64]{1,0:T(8,128)S(1)} %select_reduce_fusion.place, s32[7]{0:T(128)S(1)} %copy-done.12, s16[272,768]{1,0:T(8,128)(2,1)S(1)} %get-tuple-element.15.refs_0_, s16[272,768]{1,0:T(8,128)(2,1)} %collective-permute-done.8.refs_1_, ...), custom_call_target="tpu_custom_call" | custom-call | tf_op jit(solution)/shard_map/finish/pallas_call | solution.py:365
  190.4 0.7 copy-done.11
  191.0 1.1 collective-permute-start.15
  192.2 1.3 collective-permute-done.15
  193.5 1.9 maximum_select_fusion
  195.3 1.4 total.1
  (57 shorter events, 2.9 us)
Async XLA Ops:
  0.6 127.8 %copy-start = (f32[6,256,256]{2,1,0:T(8,128)S(1)}, f32[6,256,256]{2,1,0:T(8,128)}, u32[]{:S(2)}) copy-start(f32[6,256,256]{2,1,0:T(8,128)} %param.9) | copy-start | bytes 4718596
  0.6 77.2 %collective-permute-start = (bf16[2048,1024]{1,0:T(8,128)(2,1)}, bf16[2048,1024]{1,0:T(8,128)(2,1)}, u32[]{:S(2)}, u32[]{:S(2)}) collective-permute-start(bf16[2048,1024]{1,0:T(8,128)(2,1)} %own_ref.1), channel_id=1, source_target_pairs={{0,1},{1,0},{2,3},{3,2},{4,5},{5,4},{6,7},{7,6},{8,9},{9,8},{10,11... | collective-permute-start | bytes 12582920 | tf_op jit(solution)/shard_map/ppermute | solution.py:274
  5.5 8.1 %copy-start.14 = (s32[6,32]{1,0:T(8,128)S(1)}, s32[6,32]{1,0:T(8,128)}, u32[]{:S(2)}) copy-start(s32[6,32]{1,0:T(8,128)} %param.8) | copy-start | bytes 2308
  5.6 8.1 %copy-start.15 = (s32[6,32]{1,0:T(8,128)S(1)}, s32[6,32]{1,0:T(8,128)}, u32[]{:S(2)}) copy-start(s32[6,32]{1,0:T(8,128)} %param.7) | copy-start | bytes 2308
  5.6 30.9 %copy-start.12 = (s32[7]{0:T(128)S(1)}, s32[7]{0:T(128)}, u32[]{:S(2)}) copy-start(s32[7]{0:T(128)} %stack.31.where) | copy-start | bytes 88
  5.6 30.9 %all-to-all-start = ((bf16[16,2,3,32,256]{4,3,2,1,0:T(8,128)(2,1)}), bf16[16,2,3,32,256]{4,3,2,1,0:T(8,128)(2,1)S(1)}, u32[]{:S(2)}, u32[]{:S(2)}) async-start(bf16[16,2,3,32,256]{4,3,2,1,0:T(8,128)(2,1)} %share.1), calls=%async_computation | async-start | bytes 3145728 | tf_op jit(solution)/shard_map/all_to_all | solution.py:292
  37.3 0.7 copy-start.10
  38.0 16.1 %collective-permute-start.1 = (bf16[3,8,32,256]{3,2,1,0:T(8,128)(2,1)S(1)}, bf16[3,8,32,256]{3,2,1,0:T(8,128)(2,1)S(1)}, u32[]{:S(2)}, u32[]{:S(2)}) collective-permute-start(bf16[3,8,32,256]{3,2,1,0:T(8,128)(2,1)S(1)} %get-tuple-element.14.refs_0_), channel_id=1, source_target_pairs={{0,32},{32,64},{64,96},{96,0},{1,33},{33,65},{65,97},{97,1},{2,34}... | collective-permute-start | bytes 1179656 | tf_op jit(solution)/shard_map/ppermute | solution.py:248
  39.3 14.9 %all-to-all-start.1 = ((bf16[8,3,32,256]{3,2,1,0:T(8,128)(2,1)}), bf16[8,3,32,256]{3,2,1,0:T(8,128)(2,1)S(1)}, u32[]{:S(2)}, u32[]{:S(2)}) async-start(bf16[8,3,32,256]{3,2,1,0:T(8,128)(2,1)} %copy-done.10), calls=%async_computation.1 | async-start | bytes 786432 | tf_op jit(solution)/shard_map/all_to_all | solution.py:307
  43.4 13.8 %collective-permute-start.2 = (bf16[3,8,32,256]{3,2,1,0:T(8,128)(2,1)S(1)}, bf16[3,8,32,256]{3,2,1,0:T(8,128)(2,1)S(1)}, u32[]{:S(2)}, u32[]{:S(2)}) collective-permute-start(bf16[3,8,32,256]{3,2,1,0:T(8,128)(2,1)S(1)} %get-tuple-element.14.refs_0_), channel_id=1, source_target_pairs={{0,96},{32,0},{64,32},{96,64},{1,97},{33,1},{65,33},{97,65},{2,98}... | collective-permute-start | bytes 1179656 | tf_op jit(solution)/shard_map/ppermute | solution.py:249
  46.1 12.7 %collective-permute-start.4 = (bf16[3,8,32,256]{3,2,1,0:T(8,128)(2,1)S(1)}, bf16[3,8,32,256]{3,2,1,0:T(8,128)(2,1)}, u32[]{:S(2)}, u32[]{:S(2)}) collective-permute-start(bf16[3,8,32,256]{3,2,1,0:T(8,128)(2,1)S(1)} %get-tuple-element.14.refs_0_), channel_id=1, source_target_pairs={{0,16},{16,0},{1,17},{17,1},{2,18},{18,2},{3,19},{19,3},{4,20},{20... | collective-permute-start | bytes 1179656 | tf_op jit(solution)/shard_map/ppermute | solution.py:304
  54.1 10.0 %collective-permute-start.16 = (bf16[8,3,32,256]{3,2,1,0:T(8,128)(2,1)S(1)}, bf16[8,3,32,256]{3,2,1,0:T(8,128)(2,1)S(1)}, u32[]{:S(2)}, u32[]{:S(2)}) collective-permute-start(bf16[8,3,32,256]{3,2,1,0:T(8,128)(2,1)S(1)} %all-to-all-done.1.refs_8_), channel_id=1, source_target_pairs={{0,2},{2,4},{4,6},{6,0},{1,3},{3,5},{5,7},{7,1},{8,10},{10,12},{12... | collective-permute-start | bytes 1179656 | tf_op jit(solution)/shard_map/ppermute | solution.py:248
  54.1 30.3 %copy-start.6 = (bf16[3,8,32,256]{3,2,1,0:T(8,128)(2,1)}, bf16[3,8,32,256]{3,2,1,0:T(8,128)(2,1)S(1)}, u32[]{:S(2)}) copy-start(bf16[3,8,32,256]{3,2,1,0:T(8,128)(2,1)S(1)} %collective-permute-done.1.refs_1_) | copy-start | bytes 1179652
  54.1 13.1 %collective-permute-start.19 = (bf16[8,3,32,256]{3,2,1,0:T(8,128)(2,1)S(1)}, bf16[8,3,32,256]{3,2,1,0:T(8,128)(2,1)S(1)}, u32[]{:S(2)}, u32[]{:S(2)}) collective-permute-start(bf16[8,3,32,256]{3,2,1,0:T(8,128)(2,1)S(1)} %all-to-all-done.1.refs_8_), channel_id=1, source_target_pairs={{0,8},{8,0},{1,9},{9,1},{2,10},{10,2},{3,11},{11,3},{4,12},{12,4},... | collective-permute-start | bytes 1179656 | tf_op jit(solution)/shard_map/ppermute | solution.py:308
  57.3 27.1 %copy-start.8 = (bf16[3,8,32,256]{3,2,1,0:T(8,128)(2,1)}, bf16[3,8,32,256]{3,2,1,0:T(8,128)(2,1)S(1)}, u32[]{:S(2)}) copy-start(bf16[3,8,32,256]{3,2,1,0:T(8,128)(2,1)S(1)} %collective-permute-done.2.refs_2_) | copy-start | bytes 1179652
  57.3 10.0 %collective-permute-start.3 = (bf16[3,8,32,256]{3,2,1,0:T(8,128)(2,1)S(1)}, bf16[3,8,32,256]{3,2,1,0:T(8,128)(2,1)S(1)}, u32[]{:S(2)}, u32[]{:S(2)}) collective-permute-start(bf16[3,8,32,256]{3,2,1,0:T(8,128)(2,1)S(1)} %collective-permute-done.1.refs_1_), channel_id=1, source_target_pairs={{0,32},{32,64},{64,96},{96,0},{1,33},{33,65},{65,97},{97,1},{2,34}... | collective-permute-start | bytes 1179656 | tf_op jit(solution)/shard_map/ppermute | solution.py:250
  58.8 11.4 %collective-permute-start.6 = (bf16[3,8,32,256]{3,2,1,0:T(8,128)(2,1)}, bf16[3,8,32,256]{3,2,1,0:T(8,128)(2,1)S(1)}, u32[]{:S(2)}, u32[]{:S(2)}) collective-permute-start(bf16[3,8,32,256]{3,2,1,0:T(8,128)(2,1)} %collective-permute-done.4.refs_4_), channel_id=1, source_target_pairs={{0,96},{32,0},{64,32},{96,64},{1,97},{33,1},{65,33},{97,65},{2,98}... | collective-permute-start | bytes 1179656 | tf_op jit(solution)/shard_map/ppermute | solution.py:249
  64.2 12.1 %collective-permute-start.5 = (bf16[3,8,32,256]{3,2,1,0:T(8,128)(2,1)}, bf16[3,8,32,256]{3,2,1,0:T(8,128)(2,1)S(1)}, u32[]{:S(2)}, u32[]{:S(2)}) collective-permute-start(bf16[3,8,32,256]{3,2,1,0:T(8,128)(2,1)} %collective-permute-done.4.refs_4_), channel_id=1, source_target_pairs={{0,32},{32,64},{64,96},{96,0},{1,33},{33,65},{65,97},{97,1},{2,34}... | collective-permute-start | bytes 1179656 | tf_op jit(solution)/shard_map/ppermute | solution.py:248
  67.3 8.9 %collective-permute-start.21 = (bf16[8,3,32,256]{3,2,1,0:T(8,128)(2,1)S(1)}, bf16[8,3,32,256]{3,2,1,0:T(8,128)(2,1)S(1)}, u32[]{:S(2)}, u32[]{:S(2)}) collective-permute-start(bf16[8,3,32,256]{3,2,1,0:T(8,128)(2,1)S(1)} %collective-permute-done.19.refs_12_), channel_id=1, source_target_pairs={{0,6},{2,0},{4,2},{6,4},{1,7},{3,1},{5,3},{7,5},{8,14},{10,8},{12,... | collective-permute-start | bytes 1179656 | tf_op jit(solution)/shard_map/ppermute | solution.py:249
  67.3 27.2 %collective-permute-start.17 = (bf16[8,3,32,256]{3,2,1,0:T(8,128)(2,1)S(1)}, bf16[8,3,32,256]{3,2,1,0:T(8,128)(2,1)S(1)}, u32[]{:S(2)}, u32[]{:S(2)}) collective-permute-start(bf16[8,3,32,256]{3,2,1,0:T(8,128)(2,1)S(1)} %all-to-all-done.1.refs_8_), channel_id=1, source_target_pairs={{0,6},{2,0},{4,2},{6,4},{1,7},{3,1},{5,3},{7,5},{8,14},{10,8},{12,... | collective-permute-start | bytes 1179656 | tf_op jit(solution)/shard_map/ppermute | solution.py:249
  70.2 14.2 %collective-permute-start.7 = (bf16[3,8,32,256]{3,2,1,0:T(8,128)(2,1)S(1)}, bf16[3,8,32,256]{3,2,1,0:T(8,128)(2,1)S(1)}, u32[]{:S(2)}, u32[]{:S(2)}) collective-permute-start(bf16[3,8,32,256]{3,2,1,0:T(8,128)(2,1)S(1)} %collective-permute-done.6.refs_6_), channel_id=1, source_target_pairs={{0,96},{32,0},{64,32},{96,64},{1,97},{33,1},{65,33},{97,65},{2,98}... | collective-permute-start | bytes 1179656 | tf_op jit(solution)/shard_map/ppermute | solution.py:250
  76.2 18.4 %collective-permute-start.20 = (bf16[8,3,32,256]{3,2,1,0:T(8,128)(2,1)S(1)}, bf16[8,3,32,256]{3,2,1,0:T(8,128)(2,1)S(1)}, u32[]{:S(2)}, u32[]{:S(2)}) collective-permute-start(bf16[8,3,32,256]{3,2,1,0:T(8,128)(2,1)S(1)} %collective-permute-done.19.refs_12_), channel_id=1, source_target_pairs={{0,2},{2,4},{4,6},{6,0},{1,3},{3,5},{5,7},{7,1},{8,10},{10,12},{12... | collective-permute-start | bytes 1179656 | tf_op jit(solution)/shard_map/ppermute | solution.py:248
  76.2 18.4 %collective-permute-start.18 = (bf16[8,3,32,256]{3,2,1,0:T(8,128)(2,1)S(1)}, bf16[8,3,32,256]{3,2,1,0:T(8,128)(2,1)S(1)}, u32[]{:S(2)}, u32[]{:S(2)}) collective-permute-start(bf16[8,3,32,256]{3,2,1,0:T(8,128)(2,1)S(1)} %collective-permute-done.16.refs_9_), channel_id=1, source_target_pairs={{0,2},{2,4},{4,6},{6,0},{1,3},{3,5},{5,7},{7,1},{8,10},{10,12},{12... | collective-permute-start | bytes 1179656 | tf_op jit(solution)/shard_map/ppermute | solution.py:250
  77.8 16.9 %collective-permute-start.22 = (bf16[8,3,32,256]{3,2,1,0:T(8,128)(2,1)S(1)}, bf16[8,3,32,256]{3,2,1,0:T(8,128)(2,1)S(1)}, u32[]{:S(2)}, u32[]{:S(2)}) collective-permute-start(bf16[8,3,32,256]{3,2,1,0:T(8,128)(2,1)S(1)} %collective-permute-done.21.refs_14_), channel_id=1, source_target_pairs={{0,6},{2,0},{4,2},{6,4},{1,7},{3,1},{5,3},{7,5},{8,14},{10,8},{12,... | collective-permute-start | bytes 1179656 | tf_op jit(solution)/shard_map/ppermute | solution.py:250
  79.2 2.2 %copy-start.1 = (bf16[2048,1024]{1,0:T(8,128)(2,1)S(1)}, bf16[2048,1024]{1,0:T(8,128)(2,1)}, u32[]{:S(2)}) copy-start(bf16[2048,1024]{1,0:T(8,128)(2,1)} %own_ref.1) | copy-start | bytes 12582916
  84.4 1.0 copy-start.7
  85.4 1.0 copy-start.9
  94.5 4.0 %copy-start.2 = (s16[272,768]{1,0:T(8,128)(2,1)}, s16[272,768]{1,0:T(8,128)(2,1)S(1)}, u32[]{:S(2)}) copy-start(s16[272,768]{1,0:T(8,128)(2,1)S(1)} %get-tuple-element.21.refs_1_) | copy-start | bytes 1253380
  94.5 4.0 %copy-start.3 = (s16[272,768]{1,0:T(8,128)(2,1)}, s16[272,768]{1,0:T(8,128)(2,1)S(1)}, u32[]{:S(2)}) copy-start(s16[272,768]{1,0:T(8,128)(2,1)S(1)} %get-tuple-element.20.refs_4_) | copy-start | bytes 1253380
  94.5 4.0 %copy-start.4 = (s16[272,768]{1,0:T(8,128)(2,1)}, s16[272,768]{1,0:T(8,128)(2,1)S(1)}, u32[]{:S(2)}) copy-start(s16[272,768]{1,0:T(8,128)(2,1)S(1)} %get-tuple-element.19.refs_2_) | copy-start | bytes 1253380
  94.5 4.0 %copy-start.5 = (s16[272,768]{1,0:T(8,128)(2,1)}, s16[272,768]{1,0:T(8,128)(2,1)S(1)}, u32[]{:S(2)}) copy-start(s16[272,768]{1,0:T(8,128)(2,1)S(1)} %get-tuple-element.18.refs_7_) | copy-start | bytes 1253380
  114.8 19.9 %all-to-all-start.3 = ((s16[8,64,512]{2,1,0:T(8,128)(2,1)}), s16[8,64,512]{2,1,0:T(8,128)(2,1)S(1)}, u32[]{:S(2)}, u32[]{:S(2)}) async-start(s16[8,64,512]{2,1,0:T(8,128)(2,1)} %partial.1), calls=%async_computation.3 | async-start | bytes 1048576 | tf_op jit(solution)/shard_map/all_to_all | solution.py:392
  122.7 28.5 %collective-permute-start.8 = (s16[272,768]{1,0:T(8,128)(2,1)}, s16[272,768]{1,0:T(8,128)(2,1)}, u32[]{:S(2)}, u32[]{:S(2)}) collective-permute-start(s16[272,768]{1,0:T(8,128)(2,1)} %get-tuple-element.16.refs_6_), channel_id=1, source_target_pairs={{0,12},{2,14},{4,8},{6,10},{8,4},{10,6},{12,0},{14,2},{1,13},{3,15... | collective-permute-start | bytes 1253384 | tf_op jit(solution)/shard_map/ppermute | solution.py:363
  128.1 26.3 %collective-permute-start.9 = (s16[272,768]{1,0:T(8,128)(2,1)}, s16[272,768]{1,0:T(8,128)(2,1)}, u32[]{:S(2)}, u32[]{:S(2)}) collective-permute-start(s16[272,768]{1,0:T(8,128)(2,1)} %get-tuple-element.17.refs_5_), channel_id=1, source_target_pairs={{0,10},{2,12},{4,14},{6,8},{8,2},{10,4},{12,6},{14,0},{1,11},{3,13... | collective-permute-start | bytes 1253384 | tf_op jit(solution)/shard_map/ppermute | solution.py:363
  134.7 0.8 copy-start.13
  137.9 57.4 %all-to-all-start.4 = ((s16[16,64,512]{2,1,0:T(8,128)(2,1)}), s16[16,64,512]{2,1,0:T(8,128)(2,1)S(1)}, u32[]{:S(2)}, u32[]{:S(2)}) async-start(s16[16,64,512]{2,1,0:T(8,128)(2,1)} %piece.1), calls=%async_computation.4 | async-start | bytes 2097152 | tf_op jit(solution)/shard_map/all_to_all | solution.py:408
  150.1 21.8 %collective-permute-start.10 = (s16[272,768]{1,0:T(8,128)(2,1)}, s16[272,768]{1,0:T(8,128)(2,1)S(1)}, u32[]{:S(2)}, u32[]{:S(2)}) collective-permute-start(s16[272,768]{1,0:T(8,128)(2,1)} %copy-done.5), channel_id=1, source_target_pairs={{0,14},{2,8},{4,10},{6,12},{8,6},{10,0},{12,2},{14,4},{1,15},{3,9}... | collective-permute-start | bytes 1253384 | tf_op jit(solution)/shard_map/ppermute | solution.py:363
  150.1 21.8 %collective-permute-start.11 = (s16[272,768]{1,0:T(8,128)(2,1)}, s16[272,768]{1,0:T(8,128)(2,1)S(1)}, u32[]{:S(2)}, u32[]{:S(2)}) collective-permute-start(s16[272,768]{1,0:T(8,128)(2,1)} %copy-done.4), channel_id=1, source_target_pairs={{0,4},{2,6},{4,0},{6,2},{8,12},{10,14},{12,8},{14,10},{1,5},{3,7},... | collective-permute-start | bytes 1253384 | tf_op jit(solution)/shard_map/ppermute | solution.py:363
  151.0 30.9 %collective-permute-start.12 = (s16[272,768]{1,0:T(8,128)(2,1)}, s16[272,768]{1,0:T(8,128)(2,1)S(1)}, u32[]{:S(2)}, u32[]{:S(2)}) collective-permute-start(s16[272,768]{1,0:T(8,128)(2,1)} %copy-done.3), channel_id=1, source_target_pairs={{0,8},{2,10},{4,12},{6,14},{8,0},{10,2},{12,4},{14,6},{1,9},{3,11}... | collective-permute-start | bytes 1253384 | tf_op jit(solution)/shard_map/ppermute | solution.py:363
  151.3 30.6 %collective-permute-start.13 = (s16[272,768]{1,0:T(8,128)(2,1)}, s16[272,768]{1,0:T(8,128)(2,1)S(1)}, u32[]{:S(2)}, u32[]{:S(2)}) collective-permute-start(s16[272,768]{1,0:T(8,128)(2,1)} %copy-done.2), channel_id=1, source_target_pairs={{0,2},{2,4},{4,6},{6,0},{8,10},{10,12},{12,14},{14,8},{1,3},{3,5},... | collective-permute-start | bytes 1253384 | tf_op jit(solution)/shard_map/ppermute | solution.py:363
  154.5 33.2 %collective-permute-start.14 = (s16[272,768]{1,0:T(8,128)(2,1)S(1)}, s16[272,768]{1,0:T(8,128)(2,1)S(1)}, u32[]{:S(2)}, u32[]{:S(2)}) collective-permute-start(s16[272,768]{1,0:T(8,128)(2,1)S(1)} %get-tuple-element.22.refs_3_), channel_id=1, source_target_pairs={{0,6},{2,0},{4,2},{6,4},{8,14},{10,8},{12,10},{14,12},{1,7},{3,1},... | collective-permute-start | bytes 1253384 | tf_op jit(solution)/shard_map/ppermute | solution.py:363
  190.4 0.7 copy-start.11
  191.0 2.4 %collective-permute-start.15 = (bf16[128,768]{1,0:T(8,128)(2,1)}, bf16[128,768]{1,0:T(8,128)(2,1)S(1)}, u32[]{:S(2)}, u32[]{:S(2)}) collective-permute-start(bf16[128,768]{1,0:T(8,128)(2,1)} %get-tuple-element.24), channel_id=1, source_target_pairs={{0,1},{1,0},{2,3},{3,2},{4,5},{5,4},{6,7},{7,6},{8,9},{9,8},{10,11... | collective-permute-start | bytes 589832 | tf_op jit(solution)/shard_map/ppermute | solution.py:374
